TPU v7x, 32 devices: a whole 2x2x4 slice. The times are simulated.
32 devices in a mesh: batch: 1, seq: 32 (over z, y, x, core).
Axes of the slice: x: 2, y: 2, z: 4, core: 2. Of those that a mesh axis runs over, the one named last changes fastest.
Arguments:
- tokens: bfloat16 [304, 262144], P('batch', 'seq'), may hold values from -6 to 6
- norm_gain: float32 [2, 304], replicated, may hold values from 0.5 to 1.5
- in_weight: bfloat16 [2, 608, 304], replicated, may hold values from -0.3125 to 0.3125
- in_bias: float32 [2, 608], replicated, may hold values from -3 to 3
- out_weight: bfloat16 [2, 304, 608], replicated, may hold values from -0.25 to 0.25
- out_bias: float32 [2, 304], replicated, may hold values from -3 to 3
Outputs:
- mixed: bfloat16 [304, 262144], P('batch', 'seq')
All inputs are finite; a program needn't handle non-finite values.
Results may differ from a plain program's by a relative error of at most 0.0056.
Values may be sent and summed in bfloat16 or wider, within the bound.
A program may use at most 64 MiB of HBM per device.

v0:
```python
import functools

import jax
import jax.numpy as jnp
from jax import lax
from jax.experimental import pallas as pl
from jax.experimental.pallas import tpu as pltpu
from jax.sharding import PartitionSpec as P

TRACK_CH = 16
TRACKS = 19
BLOCKS = 2
LANES = 128
CHUNK = 2048
TILE = 2048
LAG = 2
MESH = pl.DeviceIdType.MESH


class Plan:
    def __init__(self, count, rows, chunk, tile, plane):
        self.count, self.rows, self.chunk, self.tile = count, rows, chunk, tile
        self.chunks = rows // chunk
        self.short = 0
        while self.short + 1 < TRACKS and 2**self.short < rows:
            self.short += 1
        self.near = (1 + self.short) * TRACK_CH
        self.distances = [2 ** (t - 1) // rows for t in range(1 + self.short, TRACKS)]
        self.far = len(self.distances)
        self.halo = max(2 ** (self.short - 1), LANES)
        self.pieces = []
        small = sum(1 for t in range(1, 1 + self.short) if 2 ** (t - 1) < LANES)
        self.pieces.append((TRACK_CH, small * TRACK_CH, LANES, LANES, self.chunks - 1, 0))
        for t in range(1 + small, 1 + self.short):
            offset = 2 ** (t - 1)
            width = min(offset, chunk)
            for part in range(offset // width):
                from_end = offset - part * width
                source = (rows - from_end) // chunk
                self.pieces.append((t * TRACK_CH, TRACK_CH, from_end, width, source, part))
        self.plane = plane
        self.relays = []
        if plane:
            last = plane - 1
            self.relays = [(0, last, 2, 0), (None, last, 3, 0), (1, last - 1, 0, 0), (1, last, 1, 1)]
        peers = []
        hops = [1] + self.distances
        for _, sender, relay, receiver in self.relays:
            hops += [(relay - sender) % count, (plane + receiver - relay) % count]
        for d in hops:
            for signed in (d, count - d):
                if signed % count and signed % count not in peers:
                    peers.append(signed % count)
        self.peers = peers


def rotated_tile(plan, ext, far, col):
    tile, halo = plan.tile, plan.halo
    parts = []
    for t in range(1 + plan.short):
        rows = pl.ds(t * TRACK_CH, TRACK_CH)
        offset = 0 if t == 0 else 2 ** (t - 1)
        if offset % LANES == 0:
            start = pl.multiple_of(halo - offset + col, LANES)
            parts.append(ext[rows, pl.ds(start, tile)].astype(jnp.float32))
        else:
            start = pl.multiple_of(halo - LANES + col, LANES)
            window = ext[rows, pl.ds(start, tile + LANES)].astype(jnp.float32)
            parts.append(pltpu.roll(window, offset, 1)[:, LANES:])
    parts.append(far[:, pl.ds(pl.multiple_of(col, LANES), tile)].astype(jnp.float32))
    return jnp.concatenate(parts, 0)


def columns(row):
    return jnp.broadcast_to(row, (LANES, row.shape[1])).T


def across(column, width):
    return jnp.concatenate([column] * (width // LANES), 1)


def mix_tile(as_float, gain, in_weight, in_bias, out_weight, out_bias):
    mean_square = jnp.mean(as_float * as_float, axis=0, keepdims=True)
    normed = (as_float * gain * lax.rsqrt(mean_square + 1e-06)).astype(jnp.bfloat16)
    pre_act = jnp.dot(in_weight, normed, preferred_element_type=jnp.float32) + in_bias
    inner = pre_act * (0.7978845608028654 + 0.035677408136300125 * (pre_act * pre_act))
    half = 0.5 * pre_act
    active = (half + half * jnp.tanh(inner)).astype(jnp.bfloat16)
    summed = as_float + jnp.dot(out_weight, active, preferred_element_type=jnp.float32) + out_bias
    return summed.astype(jnp.bfloat16)


def kernel(plan, tokens, gain_in, w_in_t, b_in_in, w_out, b_out_in, out,
           gain, w_in, b_in, b_out, relay_far, relay_halo, ext0, ext1, far0, far1, sent1, result,
           far_send, far_recv, halo_send, halo_recv,
           pass_send, pass_recv, pass_halo_send, pass_halo_recv, load_sem, store_sem):
    me = lax.axis_index("seq")
    chunk, tile, near, halo, rows = plan.chunk, plan.tile, plan.near, plan.halo, plan.rows
    exts, fars = (ext0, ext1), (far0, far1)

    load = pltpu.make_async_copy(tokens.at[pl.ds(0, near), :], ext0.at[:, pl.ds(halo, rows)], load_sem)
    load.start()

    barrier = pltpu.get_barrier_semaphore()
    for peer in plan.peers:
        pl.semaphore_signal(barrier, inc=1, device_id={"seq": lax.rem(me + peer, plan.count)}, device_id_type=MESH)
    pl.semaphore_wait(barrier, len(plan.peers))

    place = lax.rem(me, plan.plane) if plan.plane else me

    def along(hop):
        return {"seq": lax.rem(me + hop + plan.count, plan.count)}

    def far_copy(block, index, number, relay=None):
        cols = pl.ds(pl.multiple_of(number * chunk, LANES), chunk)
        if block == 0:
            source = tokens.at[pl.ds(near + index * TRACK_CH, TRACK_CH), cols]
        else:
            source = sent1.at[pl.ds(index * TRACK_CH, TRACK_CH), cols]
        if relay is None:
            target = fars[block].at[pl.ds(index * TRACK_CH, TRACK_CH), cols]
            arrived, hop = far_recv.at[block, index, number], plan.distances[index]
        else:
            target, arrived, hop = relay_far.at[block, :, cols], pass_recv.at[block, number], relay[2] - relay[1]
        return pltpu.make_async_remote_copy(
            src_ref=source, dst_ref=target, send_sem=far_send.at[block, index, number], recv_sem=arrived,
            device_id=along(hop), device_id_type=MESH,
        )

    def far_pass(block, relay, number):
        index, _, at, receiver = relay
        cols = pl.ds(pl.multiple_of(number * chunk, LANES), chunk)
        return pltpu.make_async_remote_copy(
            src_ref=relay_far.at[block, :, cols],
            dst_ref=fars[block].at[pl.ds(index * TRACK_CH, TRACK_CH), cols],
            send_sem=pass_send.at[block, number],
            recv_sem=far_recv.at[block, index, number],
            device_id=along(plan.plane + receiver - at), device_id_type=MESH,
        )

    def halo_copy(block, number, relay=None):
        first, height, from_end, width, _, _ = plan.pieces[number]
        where = (pl.ds(first, height), pl.ds(halo - from_end, width))
        if block == 0:
            source = tokens.at[pl.ds(first, height), pl.ds(rows - from_end, width)]
        else:
            source = ext1.at[pl.ds(first, height), pl.ds(halo + rows - from_end, width)]
        if relay is None:
            target, arrived, hop = exts[block].at[where], halo_recv.at[block, number], 1
        else:
            target, arrived = relay_halo.at[(block, *where)], pass_halo_recv.at[block, number]
            hop = relay[2] - relay[1]
        return pltpu.make_async_remote_copy(
            src_ref=source, dst_ref=target, send_sem=halo_send.at[block, number], recv_sem=arrived,
            device_id=along(hop), device_id_type=MESH,
        )

    def halo_pass(block, relay, number):
        first, height, from_end, width, _, _ = plan.pieces[number]
        where = (pl.ds(first, height), pl.ds(halo - from_end, width))
        return pltpu.make_async_remote_copy(
            src_ref=relay_halo.at[(block, *where)],
            dst_ref=exts[block].at[where],
            send_sem=pass_halo_send.at[block, number],
            recv_sem=halo_recv.at[block, number],
            device_id=along(plan.plane + relay[3] - relay[2]), device_id_type=MESH,
        )

    def start(make, key, *args):
        relays = [relay for relay in plan.relays if relay[0] == key]
        direct = place >= 0
        for relay in relays:
            direct = direct & (place != relay[1])

            @pl.when(place == relay[1])
            def _(relay=relay):
                make(*args, relay=relay).start()

        if relays:
            @pl.when(direct)
            def _():
                make(*args).start()
        else:
            make(*args).start()

    def forward(block, number, halo_of):
        for relay in plan.relays:
            @pl.when((place == relay[2]) & (number >= 0) & (number < plan.chunks))
            def _(relay=relay):
                if relay[0] is None:
                    for piece in range(len(plan.pieces)):
                        @pl.when(number == plan.pieces[piece][halo_of])
                        def _(piece=piece):
                            halo_copy(block, piece, relay).wait_recv()
                            halo_pass(block, relay, piece).start()
                else:
                    far_copy(block, relay[0], number, relay).wait_recv()
                    far_pass(block, relay, number).start()

    def store(number):
        cols = pl.ds(pl.multiple_of(number * chunk, LANES), chunk)
        return pltpu.make_async_copy(result.at[:, cols], out.at[:, cols], store_sem.at[number])

    @pl.loop(0, plan.chunks)
    def _(step):
        number = plan.chunks - 1 - step
        for index in range(plan.far):
            start(far_copy, index, 0, index, number)
        for piece, (*_, reader) in enumerate(plan.pieces):
            @pl.when(number == reader)
            def _(piece=piece):
                start(halo_copy, None, 0, piece)

    forward(0, plan.chunks - 1, 5)

    for block in range(BLOCKS):
        gain[block] = columns(gain_in[block:block + 1, :])
        b_in[block] = columns(b_in_in[block:block + 1, :])
        b_out[block] = columns(b_out_in[block:block + 1, :])
        w_in[block] = w_in_t[block].T

    load.wait()

    for block in range(BLOCKS):
        ext, far = exts[block], fars[block]

        @pl.loop(0, plan.chunks)
        def _(step, block=block, ext=ext, far=far):
            number = plan.chunks - 1 - step
            if block == 0:
                forward(0, number - 1, 5)
            forward(1, number + LAG - block * plan.chunks, 4)
            for index in range(plan.far):
                far_copy(block, index, number).wait_recv()
            for piece, (*_, reader) in enumerate(plan.pieces):
                @pl.when(number == reader)
                def _(piece=piece):
                    halo_copy(block, piece).wait_recv()

            @pl.loop(0, chunk // tile)
            def _(part):
                col = pl.multiple_of(number * chunk + part * tile, LANES)
                value = mix_tile(
                    rotated_tile(plan, ext, far, col),
                    across(gain[block], tile), w_in[block], across(b_in[block], tile),
                    w_out[block], across(b_out[block], tile),
                )
                if block + 1 < BLOCKS:
                    ext1[:, pl.ds(pl.multiple_of(halo + col, LANES), tile)] = value[:near]
                    sent1[:, pl.ds(col, tile)] = value[near:]
                else:
                    result[:, pl.ds(col, tile)] = value

            if block + 1 < BLOCKS:
                for index in range(plan.far):
                    start(far_copy, index, 1, index, number)
                for piece, (*_, source, _) in enumerate(plan.pieces):
                    @pl.when(number == source)
                    def _(piece=piece):
                        start(halo_copy, None, 1, piece)
            else:
                store(number).start()

    @pl.loop(0, plan.chunks)
    def _(number):
        for block in range(BLOCKS):
            for index in range(plan.far):
                far_copy(block, index, number).wait_send()
            for relay in plan.relays:
                if relay[0] is not None:
                    @pl.when(place == relay[2])
                    def _(relay=relay, block=block):
                        far_pass(block, relay, number).wait_send()
        store(number).wait()

    for block in range(BLOCKS):
        for piece in range(len(plan.pieces)):
            halo_copy(block, piece).wait_send()
            for relay in plan.relays:
                if relay[0] is None:
                    @pl.when(place == relay[2])
                    def _(relay=relay, block=block, piece=piece):
                        halo_pass(block, relay, piece).wait_send()


def plane_of(mesh):
    devices = mesh.devices.reshape(-1)
    if mesh.shape["seq"] != devices.size or not hasattr(devices[0], "coords"):
        return 0
    places = [(*reversed(d.coords), d.core_on_chip) for d in devices]
    shape = tuple(max(p[axis] for p in places) + 1 for axis in range(4))
    plane = shape[1] * shape[2] * shape[3]
    ordered = [(i // plane, i // 4 % 2, i // 2 % 2, i % 2) for i in range(devices.size)]
    return plane if shape[1:] == (2, 2, 2) and shape[0] > 1 and places == ordered else 0


def solution(mesh):
    count = mesh.shape["seq"]
    plane = plane_of(mesh)

    def shards(tokens, norm_gain, in_weight, in_bias, out_weight, out_bias):
        channels, rows = tokens.shape
        plan = Plan(count, rows, min(CHUNK, rows // 2), min(TILE, rows // 2), plane)
        distant = plan.far * TRACK_CH
        wide = plan.halo + rows
        vmem = pl.BlockSpec(memory_space=pltpu.VMEM)
        return pl.pallas_call(
            functools.partial(kernel, plan),
            out_shape=jax.ShapeDtypeStruct(tokens.shape, tokens.dtype),
            in_specs=[pl.BlockSpec(memory_space=pl.ANY)] + [vmem] * 5,
            out_specs=pl.BlockSpec(memory_space=pl.ANY),
            scratch_shapes=[
                pltpu.VMEM((BLOCKS, channels, LANES), jnp.float32),
                pltpu.VMEM(in_weight.shape, jnp.bfloat16),
                pltpu.VMEM((BLOCKS, in_weight.shape[1], LANES), jnp.float32),
                pltpu.VMEM((BLOCKS, channels, LANES), jnp.float32),
                pltpu.VMEM((BLOCKS, TRACK_CH, rows), jnp.bfloat16),
                pltpu.VMEM((BLOCKS, plan.near, plan.halo), jnp.bfloat16),
                pltpu.VMEM((plan.near, wide), jnp.bfloat16),
                pltpu.VMEM((plan.near, wide), jnp.bfloat16),
                pltpu.VMEM((distant, rows), jnp.bfloat16),
                pltpu.VMEM((distant, rows), jnp.bfloat16),
                pltpu.VMEM((distant, rows), jnp.bfloat16),
                pltpu.VMEM((channels, rows), jnp.bfloat16),
                pltpu.SemaphoreType.DMA((BLOCKS, plan.far, plan.chunks)),
                pltpu.SemaphoreType.DMA((BLOCKS, plan.far, plan.chunks)),
                pltpu.SemaphoreType.DMA((BLOCKS, len(plan.pieces))),
                pltpu.SemaphoreType.DMA((BLOCKS, len(plan.pieces))),
                pltpu.SemaphoreType.DMA((BLOCKS, plan.chunks)),
                pltpu.SemaphoreType.DMA((BLOCKS, plan.chunks)),
                pltpu.SemaphoreType.DMA((BLOCKS, len(plan.pieces))),
                pltpu.SemaphoreType.DMA((BLOCKS, len(plan.pieces))),
                pltpu.SemaphoreType.DMA,
                pltpu.SemaphoreType.DMA((plan.chunks,)),
            ],
            compiler_params=pltpu.CompilerParams(
                collective_id=0, has_side_effects=True, vmem_limit_bytes=56 * 2**20
            ),
        )(tokens, norm_gain, jnp.swapaxes(in_weight, 1, 2), in_bias, out_weight, out_bias)

    return jax.shard_map(
        shards,
        mesh=mesh,
        in_specs=(P("batch", "seq"), P(), P(), P(), P(), P()),
        out_specs=P("batch", "seq"),
        check_vma=False,
    )
```

profile of v0, /device:TPU:8, one launch (start us, length us, event | category | flops | bytes accessed | tf_op | source)
XLA Modules:
  0.0 81.2 jit_solution(15625685971469756393)
XLA Ops:
  0.0 76.0 %shard_map.64 = bf16[304,8192]{1,0:T(8,128)(2,1)} custom-call(bf16[304,8192]{1,0:T(8,128)(2,1)} %tokens.1, f32[2,304]{1,0:T(2,128)} %gain_in.1, bf16[2,304,608]{2,1,0:T(8,128)(2,1)} %bitcast.1, f32[2,608]{1,0:T(2,128)} %b_in_in.1, bf16[2,304,608]{2,1,0:T(8,128)(2,1)} %w_out.1, f32[2,304]{1,0:T(2,128)} %b_out_in.1), custom_call_target="tpu_custom_call" | custom-call | tf_op jit(solution)/shard_map/pallas_call | solution.py:307
  76.0 5.2 %copy.8 = bf16[304,8192]{1,0:T(8,128)(2,1)} copy(bf16[304,8192]{1,0:T(8,128)(2,1)} %shard_map.64) | data formatting | bytes 9961472
where the time goes:
time: 81.4 us; the launch traced here: 81.2 us
  Pallas kernels  76 us (93%)
  local copies, waits for them, and re-layouts  5.22 us (6%)
    pallas_call x1, Pallas kernels, shards(): pl.pallas_call(functools.partial(kernel, plan), out_shape=jax.ShapeDtypeS...  76 us
    unnamed x1, local copies, waits for them, and re-layouts  5.22 us

commit v1 on v0

--- a/solution.py
+++ b/solution.py
@@ -11,15 +11,16 @@
 TRACKS = 19
 BLOCKS = 2
 LANES = 128
-CHUNK = 2048
-TILE = 2048
+CHUNK = 1024
 LAG = 2
+AHEAD = 1
+WINDOW = 3
 MESH = pl.DeviceIdType.MESH
 
 
 class Plan:
-    def __init__(self, count, rows, chunk, tile, plane):
-        self.count, self.rows, self.chunk, self.tile = count, rows, chunk, tile
+    def __init__(self, count, rows, chunk, plane):
+        self.count, self.rows, self.chunk = count, rows, chunk
         self.chunks = rows // chunk
         self.short = 0
         while self.short + 1 < TRACKS and 2**self.short < rows:
@@ -38,6 +39,12 @@
                 from_end = offset - part * width
                 source = (rows - from_end) // chunk
                 self.pieces.append((t * TRACK_CH, TRACK_CH, from_end, width, source, part))
+        self.pieces.sort(key=lambda piece: (-piece[5], piece[2] if piece[3] < chunk else -piece[2]))
+        big = [piece for piece in self.pieces if piece[1] * piece[3] >= TRACK_CH * chunk]
+        self.pieces = big + [piece for piece in self.pieces if piece not in big]
+        self.steps = [
+            max(min(at, self.chunks - 1), self.chunks - 1 - piece[4]) for at, piece in enumerate(self.pieces)
+        ]
         self.plane = plane
         self.relays = []
         if plane:
@@ -55,7 +62,7 @@
 
 
 def rotated_tile(plan, ext, far, col):
-    tile, halo = plan.tile, plan.halo
+    tile, halo = plan.chunk, plan.halo
     parts = []
     for t in range(1 + plan.short):
         rows = pl.ds(t * TRACK_CH, TRACK_CH)
@@ -90,16 +97,24 @@
     return summed.astype(jnp.bfloat16)
 
 
-def kernel(plan, tokens, gain_in, w_in_t, b_in_in, w_out, b_out_in, out,
-           gain, w_in, b_in, b_out, relay_far, relay_halo, ext0, ext1, far0, far1, sent1, result,
+def kernel(plan, tokens, gain_in, w_in_in, b_in_in, w_out_in, b_out_in, out,
+           gain_row, w_in_t, b_in_row, w_out, b_out_row, gain, w_in, b_in, b_out,
+           relay_far, relay_halo, ext0, ext1, far0, far1, sent1,
            far_send, far_recv, halo_send, halo_recv,
-           pass_send, pass_recv, pass_halo_send, pass_halo_recv, load_sem, store_sem):
+           pass_send, pass_recv, pass_halo_send, pass_halo_recv, load_sem):
     me = lax.axis_index("seq")
-    chunk, tile, near, halo, rows = plan.chunk, plan.tile, plan.near, plan.halo, plan.rows
+    chunk, near, halo, rows = plan.chunk, plan.near, plan.halo, plan.rows
     exts, fars = (ext0, ext1), (far0, far1)
 
-    load = pltpu.make_async_copy(tokens.at[pl.ds(0, near), :], ext0.at[:, pl.ds(halo, rows)], load_sem)
-    load.start()
+    loads = [
+        pltpu.make_async_copy(source, target, load_sem.at[at])
+        for at, (source, target) in enumerate((
+            (gain_in, gain_row), (w_in_in, w_in_t), (b_in_in, b_in_row), (w_out_in, w_out), (b_out_in, b_out_row),
+            (tokens.at[pl.ds(0, near), :], ext0.at[:, pl.ds(halo, rows)]),
+        ))
+    ]
+    for load in loads:
+        load.start()
 
     barrier = pltpu.get_barrier_semaphore()
     for peer in plan.peers:
@@ -166,60 +181,98 @@
             device_id=along(plan.plane + relay[3] - relay[2]), device_id_type=MESH,
         )
 
-    def start(make, key, *args):
+    def start(make, key, *args, direct=True, relayed=True):
         relays = [relay for relay in plan.relays if relay[0] == key]
-        direct = place >= 0
-        for relay in relays:
-            direct = direct & (place != relay[1])
-
-            @pl.when(place == relay[1])
-            def _(relay=relay):
-                make(*args, relay=relay).start()
-
-        if relays:
-            @pl.when(direct)
+        if relayed:
+            for relay in relays:
+                @pl.when(place == relay[1])
+                def _(relay=relay):
+                    make(*args, relay=relay).start()
+
+        if direct and relays:
+            own = place >= 0
+            for relay in relays:
+                own = own & (place != relay[1])
+
+            @pl.when(own)
             def _():
                 make(*args).start()
-        else:
+        elif direct:
             make(*args).start()
 
-    def forward(block, number, halo_of):
+    def send(block, step, **kinds):
+        for index in reversed(range(plan.far)):
+            start(far_copy, index, block, index, plan.chunks - 1 - step, **kinds)
+        for piece, at in enumerate(plan.steps):
+            @pl.when(step == at)
+            def _(piece=piece):
+                start(halo_copy, None, block, piece, **kinds)
+
+    def pass_far(block, number):
         for relay in plan.relays:
-            @pl.when((place == relay[2]) & (number >= 0) & (number < plan.chunks))
-            def _(relay=relay):
-                if relay[0] is None:
-                    for piece in range(len(plan.pieces)):
-                        @pl.when(number == plan.pieces[piece][halo_of])
-                        def _(piece=piece):
-                            halo_copy(block, piece, relay).wait_recv()
-                            halo_pass(block, relay, piece).start()
-                else:
+            if relay[0] is not None:
+                @pl.when(place == relay[2])
+                def _(relay=relay):
                     far_copy(block, relay[0], number, relay).wait_recv()
                     far_pass(block, relay, number).start()
 
-    def store(number):
-        cols = pl.ds(pl.multiple_of(number * chunk, LANES), chunk)
-        return pltpu.make_async_copy(result.at[:, cols], out.at[:, cols], store_sem.at[number])
-
-    @pl.loop(0, plan.chunks)
+    def pass_halo(block, piece):
+        for relay in plan.relays:
+            if relay[0] is None:
+                @pl.when(place == relay[2])
+                def _(relay=relay):
+                    halo_copy(block, piece, relay).wait_recv()
+                    halo_pass(block, relay, piece).start()
+
+    def hand_on(block, step):
+        pass_far(block, plan.chunks - 1 - step)
+        for piece, at in enumerate(plan.steps):
+            @pl.when(step == at)
+            def _(piece=piece):
+                pass_halo(block, piece)
+
+    def at_step(block, step, action, *conditions, **kinds):
+        for b in range(BLOCKS):
+            if b < block:
+                continue
+            own = step - (b - block) * plan.chunks
+            fits = (own >= 0) & (own < plan.chunks)
+            for condition in conditions:
+                fits = fits & condition
+
+            @pl.when(fits)
+            def _(b=b, own=own):
+                action(b, own, **kinds)
+
+    paced = me >= plan.count - plan.plane
+    free = me < plan.count - plan.plane
+    window = min(WINDOW, plan.chunks - 1)
+
+    @pl.loop(0, plan.chunks + AHEAD)
     def _(step):
-        number = plan.chunks - 1 - step
-        for index in range(plan.far):
-            start(far_copy, index, 0, index, number)
-        for piece, (*_, reader) in enumerate(plan.pieces):
-            @pl.when(number == reader)
-            def _(piece=piece):
-                start(halo_copy, None, 0, piece)
-
-    forward(0, plan.chunks - 1, 5)
+        within = (step < window) | free
+
+        @pl.when((step < plan.chunks) & within)
+        def _():
+            send(0, step)
+
+        if plan.plane:
+            @pl.when((step == window) & paced)
+            def _():
+                send(0, step, direct=False)
+
+            @pl.when((step >= AHEAD) & ((step - AHEAD < window) | free))
+            def _():
+                hand_on(0, step - AHEAD)
+
+    for load in loads:
+        load.wait()
 
     for block in range(BLOCKS):
-        gain[block] = columns(gain_in[block:block + 1, :])
-        b_in[block] = columns(b_in_in[block:block + 1, :])
-        b_out[block] = columns(b_out_in[block:block + 1, :])
+        gain[block] = columns(gain_row[block:block + 1, :])
+        b_in[block] = columns(b_in_row[block:block + 1, :])
+        b_out[block] = columns(b_out_row[block:block + 1, :])
         w_in[block] = w_in_t[block].T
-
-    load.wait()
 
     for block in range(BLOCKS):
         ext, far = exts[block], fars[block]
@@ -227,9 +280,13 @@
         @pl.loop(0, plan.chunks)
         def _(step, block=block, ext=ext, far=far):
             number = plan.chunks - 1 - step
-            if block == 0:
-                forward(0, number - 1, 5)
-            forward(1, number + LAG - block * plan.chunks, 4)
+            if plan.plane:
+                ready = step - LAG + block * plan.chunks
+
+                @pl.when(free & (ready >= 0) & (ready < plan.chunks))
+                def _():
+                    hand_on(1, ready)
+
             for index in range(plan.far):
                 far_copy(block, index, number).wait_recv()
             for piece, (*_, reader) in enumerate(plan.pieces):
@@ -237,29 +294,26 @@
                 def _(piece=piece):
                     halo_copy(block, piece).wait_recv()
 
-            @pl.loop(0, chunk // tile)
-            def _(part):
-                col = pl.multiple_of(number * chunk + part * tile, LANES)
-                value = mix_tile(
-                    rotated_tile(plan, ext, far, col),
-                    across(gain[block], tile), w_in[block], across(b_in[block], tile),
-                    w_out[block], across(b_out[block], tile),
-                )
-                if block + 1 < BLOCKS:
-                    ext1[:, pl.ds(pl.multiple_of(halo + col, LANES), tile)] = value[:near]
-                    sent1[:, pl.ds(col, tile)] = value[near:]
-                else:
-                    result[:, pl.ds(col, tile)] = value
-
+            if plan.plane:
+                at_step(block, step + window, hand_on, paced)
+                at_step(block, step + window, send, paced, relayed=False)
+                at_step(block, step + window + 1, send, paced, direct=False)
+
+            col = pl.multiple_of(number * chunk, LANES)
+            value = mix_tile(
+                rotated_tile(plan, ext, far, col),
+                across(gain[block], chunk), w_in[block], across(b_in[block], chunk),
+                w_out[block], across(b_out[block], chunk),
+            )
             if block + 1 < BLOCKS:
-                for index in range(plan.far):
-                    start(far_copy, index, 1, index, number)
-                for piece, (*_, source, _) in enumerate(plan.pieces):
-                    @pl.when(number == source)
-                    def _(piece=piece):
-                        start(halo_copy, None, 1, piece)
+                ext1[:, pl.ds(pl.multiple_of(halo + col, LANES), chunk)] = value[:near]
+                sent1[:, pl.ds(col, chunk)] = value[near:]
+
+                @pl.when(free)
+                def _():
+                    send(1, step)
             else:
-                store(number).start()
+                out[:, pl.ds(col, chunk)] = value
 
     @pl.loop(0, plan.chunks)
     def _(number):
@@ -271,7 +325,6 @@
                     @pl.when(place == relay[2])
                     def _(relay=relay, block=block):
                         far_pass(block, relay, number).wait_send()
-        store(number).wait()
 
     for block in range(BLOCKS):
         for piece in range(len(plan.pieces)):
@@ -300,16 +353,20 @@
 
     def shards(tokens, norm_gain, in_weight, in_bias, out_weight, out_bias):
         channels, rows = tokens.shape
-        plan = Plan(count, rows, min(CHUNK, rows // 2), min(TILE, rows // 2), plane)
+        plan = Plan(count, rows, min(CHUNK, rows // 2), plane)
         distant = plan.far * TRACK_CH
         wide = plan.halo + rows
-        vmem = pl.BlockSpec(memory_space=pltpu.VMEM)
+        held = [
+            pltpu.with_memory_space_constraint(x, pltpu.HBM)
+            for x in (tokens, norm_gain, jnp.swapaxes(in_weight, 1, 2), in_bias, out_weight, out_bias)
+        ]
         return pl.pallas_call(
             functools.partial(kernel, plan),
-            out_shape=jax.ShapeDtypeStruct(tokens.shape, tokens.dtype),
-            in_specs=[pl.BlockSpec(memory_space=pl.ANY)] + [vmem] * 5,
-            out_specs=pl.BlockSpec(memory_space=pl.ANY),
+            out_shape=pltpu.VMEM(tokens.shape, tokens.dtype),
+            in_specs=[pl.BlockSpec(memory_space=pl.ANY)] * len(held),
+            out_specs=pl.BlockSpec(memory_space=pltpu.VMEM),
             scratch_shapes=[
+                *(pltpu.VMEM(x.shape, x.dtype) for x in held[1:]),
                 pltpu.VMEM((BLOCKS, channels, LANES), jnp.float32),
                 pltpu.VMEM(in_weight.shape, jnp.bfloat16),
                 pltpu.VMEM((BLOCKS, in_weight.shape[1], LANES), jnp.float32),
@@ -321,7 +378,6 @@
                 pltpu.VMEM((distant, rows), jnp.bfloat16),
                 pltpu.VMEM((distant, rows), jnp.bfloat16),
                 pltpu.VMEM((distant, rows), jnp.bfloat16),
-                pltpu.VMEM((channels, rows), jnp.bfloat16),
                 pltpu.SemaphoreType.DMA((BLOCKS, plan.far, plan.chunks)),
                 pltpu.SemaphoreType.DMA((BLOCKS, plan.far, plan.chunks)),
                 pltpu.SemaphoreType.DMA((BLOCKS, len(plan.pieces))),
@@ -330,13 +386,12 @@
                 pltpu.SemaphoreType.DMA((BLOCKS, plan.chunks)),
                 pltpu.SemaphoreType.DMA((BLOCKS, len(plan.pieces))),
                 pltpu.SemaphoreType.DMA((BLOCKS, len(plan.pieces))),
-                pltpu.SemaphoreType.DMA,
-                pltpu.SemaphoreType.DMA((plan.chunks,)),
+                pltpu.SemaphoreType.DMA((len(held),)),
             ],
             compiler_params=pltpu.CompilerParams(
-                collective_id=0, has_side_effects=True, vmem_limit_bytes=56 * 2**20
+                collective_id=0, has_side_effects=True, vmem_limit_bytes=52 * 2**20
             ),
-        )(tokens, norm_gain, jnp.swapaxes(in_weight, 1, 2), in_bias, out_weight, out_bias)
+        )(*held)
 
     return jax.shard_map(
         shards,

time: 81.4 us -> 65.8 us (0.81)
  the two profiles are of different devices: /device:TPU:8 before, /device:TPU:0 now
where the time goes in v1:
time: 65.8 us; the launch traced here: 64.8 us
  Pallas kernels  62.5 us (95%)
  local copies, waits for them, and re-layouts  2.27 us (3%)
    pallas_call x1, Pallas kernels, shards(): pl.pallas_call(functools.partial(kernel, plan), out_shape=pltpu.VMEM(toke...  62.5 us
    unnamed x1, local copies, waits for them, and re-layouts  2.27 us

profile of v1, /device:TPU:0, one launch (start us, length us, event | category | flops | bytes accessed | tf_op | source)
XLA Modules:
  0.0 64.8 jit_solution(7262449015392213101)
XLA Ops:
  0.0 62.5 %shard_map.64 = bf16[304,8192]{1,0:T(8,128)(2,1)S(1)} custom-call(bf16[304,8192]{1,0:T(8,128)(2,1)} %tokens.1, f32[2,304]{1,0:T(2,128)} %gain_in.1, bf16[2,304,608]{2,1,0:T(8,128)(2,1)} %bitcast.1, f32[2,608]{1,0:T(2,128)} %b_in_in.1, bf16[2,304,608]{2,1,0:T(8,128)(2,1)} %w_out_in.1, f32[2,304]{1,0:T(2,128)} %b_out_in.1), custom_call_target="tpu_custom_call" | custom-call | tf_op jit(solution)/shard_map/pallas_call | solution.py:363
  62.5 2.3 %copy.8 = bf16[304,8192]{1,0:T(8,128)(2,1)} copy(bf16[304,8192]{1,0:T(8,128)(2,1)S(1)} %shard_map.64) | data formatting | bytes 9961472

commit v2 on v1

--- a/solution.py
+++ b/solution.py
@@ -14,7 +14,7 @@
 CHUNK = 1024
 LAG = 2
 AHEAD = 1
-WINDOW = 3
+WINDOW = 2
 MESH = pl.DeviceIdType.MESH
 
 

time: 65.8 us -> 60.7 us (0.922); the launches traced: 64.8 us -> 60.6 us
  Pallas kernels: 62.5 us -> 58.3 us
    pallas_call x1, Pallas kernels: 62.5 us -> 58.3 us  [shards(): pl.pallas_call(functools.partial(kernel, plan), out_shape=pltpu.VMEM(toke...]
where the time goes in v2:
time: 60.7 us; the launch traced here: 60.6 us
  Pallas kernels  58.3 us (96%)
  local copies, waits for them, and re-layouts  2.27 us (4%)
    pallas_call x1, Pallas kernels, shards(): pl.pallas_call(functools.partial(kernel, plan), out_shape=pltpu.VMEM(toke...  58.3 us
    unnamed x1, local copies, waits for them, and re-layouts  2.27 us

profile of v2, /device:TPU:0, one launch (start us, length us, event | category | flops | bytes accessed | tf_op | source)
XLA Modules:
  0.0 60.6 jit_solution(8229645600001747807)
XLA Ops:
  0.0 58.3 %shard_map.64 = bf16[304,8192]{1,0:T(8,128)(2,1)S(1)} custom-call(bf16[304,8192]{1,0:T(8,128)(2,1)} %tokens.1, f32[2,304]{1,0:T(2,128)} %gain_in.1, bf16[2,304,608]{2,1,0:T(8,128)(2,1)} %bitcast.1, f32[2,608]{1,0:T(2,128)} %b_in_in.1, bf16[2,304,608]{2,1,0:T(8,128)(2,1)} %w_out_in.1, f32[2,304]{1,0:T(2,128)} %b_out_in.1), custom_call_target="tpu_custom_call" | custom-call | tf_op jit(solution)/shard_map/pallas_call | solution.py:363
  58.3 2.3 %copy.8 = bf16[304,8192]{1,0:T(8,128)(2,1)} copy(bf16[304,8192]{1,0:T(8,128)(2,1)S(1)} %shard_map.64) | data formatting | bytes 9961472

commit v3 on v2

--- a/solution.py
+++ b/solution.py
@@ -14,7 +14,7 @@
 CHUNK = 1024
 LAG = 2
 AHEAD = 1
-WINDOW = 2
+STAGES = ((0, 2),)
 MESH = pl.DeviceIdType.MESH
 
 
@@ -39,12 +39,13 @@
                 from_end = offset - part * width
                 source = (rows - from_end) // chunk
                 self.pieces.append((t * TRACK_CH, TRACK_CH, from_end, width, source, part))
-        self.pieces.sort(key=lambda piece: (-piece[5], piece[2] if piece[3] < chunk else -piece[2]))
-        big = [piece for piece in self.pieces if piece[1] * piece[3] >= TRACK_CH * chunk]
-        self.pieces = big + [piece for piece in self.pieces if piece not in big]
-        self.steps = [
-            max(min(at, self.chunks - 1), self.chunks - 1 - piece[4]) for at, piece in enumerate(self.pieces)
-        ]
+        self.pieces.sort(key=lambda piece: (piece[1] * piece[3] >= TRACK_CH * chunk, -piece[0], -piece[5], piece[2]))
+        held, self.steps = 0, []
+        for piece in self.pieces:
+            self.steps.append(max(held // (TRACK_CH * chunk), self.chunks - 1 - piece[4]))
+            held += piece[1] * piece[3]
+        ends = [first for first, _ in STAGES[1:]] + [BLOCKS * self.chunks]
+        self.stages = [(first, min(end, BLOCKS * self.chunks), width) for (first, width), end in zip(STAGES, ends)]
         self.plane = plane
         self.relays = []
         if plane:
@@ -97,8 +98,8 @@
     return summed.astype(jnp.bfloat16)
 
 
-def kernel(plan, tokens, gain_in, w_in_in, b_in_in, w_out_in, b_out_in, out,
-           gain_row, w_in_t, b_in_row, w_out, b_out_row, gain, w_in, b_in, b_out,
+def kernel(plan, tokens, gain_in, w_in_in, b_in_in, w_out_in, b_out_in, out, last, gain, w_in, b_in, w_out, b_out,
+           gain_row, w_in_t, b_in_row, b_out_row,
            relay_far, relay_halo, ext0, ext1, far0, far1, sent1,
            far_send, far_recv, halo_send, halo_recv,
            pass_send, pass_recv, pass_halo_send, pass_halo_recv, load_sem):
@@ -231,37 +232,37 @@
             def _(piece=piece):
                 pass_halo(block, piece)
 
-    def at_step(block, step, action, *conditions, **kinds):
-        for b in range(BLOCKS):
-            if b < block:
-                continue
-            own = step - (b - block) * plan.chunks
-            fits = (own >= 0) & (own < plan.chunks)
-            for condition in conditions:
-                fits = fits & condition
-
-            @pl.when(fits)
-            def _(b=b, own=own):
-                action(b, own, **kinds)
+    def at_stage(block, step, lead, action, **kinds):
+        for first, end, width in plan.stages:
+            at = block * plan.chunks + step + width + lead
+            for b in range(block, BLOCKS):
+                low, high = max(first, b * plan.chunks), min(end, (b + 1) * plan.chunks)
+                if low < high:
+                    @pl.when(paced & (at >= low) & (at < high))
+                    def _(b=b, at=at):
+                        action(b, at - b * plan.chunks, **kinds)
 
     paced = me >= plan.count - plan.plane
     free = me < plan.count - plan.plane
-    window = min(WINDOW, plan.chunks - 1)
 
     @pl.loop(0, plan.chunks + AHEAD)
     def _(step):
-        within = (step < window) | free
-
-        @pl.when((step < plan.chunks) & within)
+        @pl.when((step < plan.chunks) & free)
         def _():
             send(0, step)
 
         if plan.plane:
-            @pl.when((step == window) & paced)
+            width = plan.stages[0][2]
+
+            @pl.when((step < width) & paced)
+            def _():
+                send(0, step, relayed=False)
+
+            @pl.when((step < width + 1) & paced)
             def _():
                 send(0, step, direct=False)
 
-            @pl.when((step >= AHEAD) & ((step - AHEAD < window) | free))
+            @pl.when((step >= AHEAD) & (step - AHEAD < plan.chunks) & ((step - AHEAD < width) | free))
             def _():
                 hand_on(0, step - AHEAD)
 
@@ -277,8 +278,7 @@
     for block in range(BLOCKS):
         ext, far = exts[block], fars[block]
 
-        @pl.loop(0, plan.chunks)
-        def _(step, block=block, ext=ext, far=far):
+        def advance(step, block=block, ext=ext, far=far, final=False):
             number = plan.chunks - 1 - step
             if plan.plane:
                 ready = step - LAG + block * plan.chunks
@@ -295,9 +295,13 @@
                     halo_copy(block, piece).wait_recv()
 
             if plan.plane:
-                at_step(block, step + window, hand_on, paced)
-                at_step(block, step + window, send, paced, relayed=False)
-                at_step(block, step + window + 1, send, paced, direct=False)
+                at_stage(block, step, 0, hand_on)
+                at_stage(block, step, 0, send, relayed=False)
+                at_stage(block, step, 1, send, direct=False)
+
+            if final:
+                last[...] = rotated_tile(plan, ext, far, 0).astype(jnp.bfloat16)
+                return
 
             col = pl.multiple_of(number * chunk, LANES)
             value = mix_tile(
@@ -314,6 +318,12 @@
                     send(1, step)
             else:
                 out[:, pl.ds(col, chunk)] = value
+
+        if block + 1 < BLOCKS:
+            pl.loop(0, plan.chunks)(advance)
+        else:
+            pl.loop(0, plan.chunks - 1)(advance)
+            advance(plan.chunks - 1, final=True)
 
     @pl.loop(0, plan.chunks)
     def _(number):
@@ -336,6 +346,22 @@
                         halo_pass(block, relay, piece).wait_send()
 
 
+def finish(chunk, done, last, gain, w_in, b_in, w_out, b_out, out, tail, sems):
+    rest = pl.ds(chunk, done.shape[1] - chunk)
+    body = pltpu.make_async_copy(done.at[:, rest], out.at[:, rest], sems.at[0])
+    body.start()
+    block = BLOCKS - 1
+    tail[...] = mix_tile(
+        last[...].astype(jnp.float32),
+        across(gain[block], chunk), w_in[block], across(b_in[block], chunk),
+        w_out[block], across(b_out[block], chunk),
+    )
+    end = pltpu.make_async_copy(tail, out.at[:, pl.ds(0, chunk)], sems.at[1])
+    end.start()
+    body.wait()
+    end.wait()
+
+
 def plane_of(mesh):
     devices = mesh.devices.reshape(-1)
     if mesh.shape["seq"] != devices.size or not hasattr(devices[0], "coords"):
@@ -360,17 +386,21 @@
             pltpu.with_memory_space_constraint(x, pltpu.HBM)
             for x in (tokens, norm_gain, jnp.swapaxes(in_weight, 1, 2), in_bias, out_weight, out_bias)
         ]
-        return pl.pallas_call(
+        kept = pl.pallas_call(
             functools.partial(kernel, plan),
-            out_shape=pltpu.VMEM(tokens.shape, tokens.dtype),
-            in_specs=[pl.BlockSpec(memory_space=pl.ANY)] * len(held),
-            out_specs=pl.BlockSpec(memory_space=pltpu.VMEM),
-            scratch_shapes=[
-                *(pltpu.VMEM(x.shape, x.dtype) for x in held[1:]),
+            out_shape=[
+                pltpu.VMEM(tokens.shape, tokens.dtype),
+                pltpu.VMEM((channels, plan.chunk), tokens.dtype),
                 pltpu.VMEM((BLOCKS, channels, LANES), jnp.float32),
                 pltpu.VMEM(in_weight.shape, jnp.bfloat16),
                 pltpu.VMEM((BLOCKS, in_weight.shape[1], LANES), jnp.float32),
+                pltpu.VMEM(out_weight.shape, jnp.bfloat16),
                 pltpu.VMEM((BLOCKS, channels, LANES), jnp.float32),
+            ],
+            in_specs=[pl.BlockSpec(memory_space=pl.ANY)] * len(held),
+            out_specs=[pl.BlockSpec(memory_space=pltpu.VMEM)] * 7,
+            scratch_shapes=[
+                *(pltpu.VMEM(held[at].shape, held[at].dtype) for at in (1, 2, 3, 5)),
                 pltpu.VMEM((BLOCKS, TRACK_CH, rows), jnp.bfloat16),
                 pltpu.VMEM((BLOCKS, plan.near, plan.halo), jnp.bfloat16),
                 pltpu.VMEM((plan.near, wide), jnp.bfloat16),
@@ -389,9 +419,20 @@
                 pltpu.SemaphoreType.DMA((len(held),)),
             ],
             compiler_params=pltpu.CompilerParams(
-                collective_id=0, has_side_effects=True, vmem_limit_bytes=52 * 2**20
+                collective_id=0, has_side_effects=True, vmem_limit_bytes=46 * 2**20
             ),
         )(*held)
+        return pl.pallas_call(
+            functools.partial(finish, plan.chunk),
+            out_shape=jax.ShapeDtypeStruct(tokens.shape, tokens.dtype),
+            in_specs=[pl.BlockSpec(memory_space=pltpu.VMEM)] * len(kept),
+            out_specs=pl.BlockSpec(memory_space=pl.ANY),
+            scratch_shapes=[
+                pltpu.VMEM((channels, plan.chunk), tokens.dtype),
+                pltpu.SemaphoreType.DMA((2,)),
+            ],
+            compiler_params=pltpu.CompilerParams(vmem_limit_bytes=14 * 2**20),
+        )(*kept)
 
     return jax.shard_map(
         shards,

time: 60.7 us -> 59.4 us (0.979)
  local copies, waits for them, and re-layouts: 2.27 us -> 0 us
  Pallas kernels: 58.3 us -> 59.2 us
    unnamed x1 -> x0, local copies, waits for them, and re-layouts: 2.27 us -> none
    pallas_call x1 -> x2, Pallas kernels: 58.3 us -> 59.2 us  [the longest x1 56.7 us: shards(): pl.pallas_call(functools.partial(kernel, plan), out_shape=[pltpu.VMEM(tok...]
where the time goes in v3:
time: 59.4 us; the launch traced here: 59.2 us
  Pallas kernels  59.2 us (100%)
    pallas_call x1, Pallas kernels, shards(): pl.pallas_call(functools.partial(kernel, plan), out_shape=[pltpu.VMEM(tok...  56.7 us
    pallas_call x1, Pallas kernels, shards(): pl.pallas_call(functools.partial(finish, plan.chunk), out_shape=jax.Shape...  2.48 us

profile of v3, /device:TPU:0, one launch (start us, length us, event | category | flops | bytes accessed | tf_op | source)
XLA Modules:
  0.0 59.2 jit_solution(5342735519045644023)
XLA Ops:
  0.0 56.7 %shard_map.64 = (bf16[304,8192]{1,0:T(8,128)(2,1)S(1)}, bf16[304,1024]{1,0:T(8,128)(2,1)S(1)}, f32[2,304,128]{2,1,0:T(8,128)S(1)}, bf16[2,608,304]{2,1,0:T(8,128...) custom-call(bf16[304,8192]{1,0:T(8,128)(2,1)} %tokens.1, ...), custom_call_target="tpu_custom_call" | custom-call | tf_op jit(solution)/shard_map/pallas_call | solution.py:389
  56.7 2.5 %shard_map.65 = bf16[304,8192]{1,0:T(8,128)(2,1)} custom-call(bf16[304,8192]{1,0:T(8,128)(2,1)S(1)} %get-tuple-element.12.done, bf16[304,1024]{1,0:T(8,128)(2,1)S(1)} %get-tuple-element.13.last, f32[2,304,128]{2,1,0:T(8,128)S(1)} %get-tuple-element.14.gain, bf16[2,608,304]{2,1,0:T(8,128)(2,1)S(1)} %get-tuple-element.15.w_in, ...), custom_call_target="tpu_custom_call" | custom-call | tf_op jit(solution)/shard_map/pallas_call | solution.py:425

commit v4 on v3

--- a/solution.py
+++ b/solution.py
@@ -14,6 +14,7 @@
 CHUNK = 1024
 LAG = 2
 AHEAD = 1
+HELD = 4
 STAGES = ((0, 2),)
 MESH = pl.DeviceIdType.MESH
 
@@ -275,6 +276,24 @@
         b_out[block] = columns(b_out_row[block:block + 1, :])
         w_in[block] = w_in_t[block].T
 
+    def drain(block, number):
+        for index in range(plan.far):
+            far_copy(block, index, number).wait_send()
+        for relay in plan.relays:
+            if relay[0] is not None:
+                @pl.when(place == relay[2])
+                def _(relay=relay):
+                    far_pass(block, relay, number).wait_send()
+
+    def drain_halo(block):
+        for piece in range(len(plan.pieces)):
+            halo_copy(block, piece).wait_send()
+            for relay in plan.relays:
+                if relay[0] is None:
+                    @pl.when(place == relay[2])
+                    def _(relay=relay, piece=piece):
+                        halo_pass(block, relay, piece).wait_send()
+
     for block in range(BLOCKS):
         ext, far = exts[block], fars[block]
 
@@ -318,6 +337,15 @@
                     send(1, step)
             else:
                 out[:, pl.ds(col, chunk)] = value
+                drain(0, number)
+
+                @pl.when(step == 0)
+                def _():
+                    drain_halo(0)
+
+                @pl.when(step >= HELD)
+                def _():
+                    drain(1, number + HELD)
 
         if block + 1 < BLOCKS:
             pl.loop(0, plan.chunks)(advance)
@@ -325,25 +353,9 @@
             pl.loop(0, plan.chunks - 1)(advance)
             advance(plan.chunks - 1, final=True)
 
-    @pl.loop(0, plan.chunks)
-    def _(number):
-        for block in range(BLOCKS):
-            for index in range(plan.far):
-                far_copy(block, index, number).wait_send()
-            for relay in plan.relays:
-                if relay[0] is not None:
-                    @pl.when(place == relay[2])
-                    def _(relay=relay, block=block):
-                        far_pass(block, relay, number).wait_send()
-
-    for block in range(BLOCKS):
-        for piece in range(len(plan.pieces)):
-            halo_copy(block, piece).wait_send()
-            for relay in plan.relays:
-                if relay[0] is None:
-                    @pl.when(place == relay[2])
-                    def _(relay=relay, block=block, piece=piece):
-                        halo_pass(block, relay, piece).wait_send()
+    drain(0, 0)
+    pl.loop(0, min(HELD + 1, plan.chunks))(functools.partial(drain, 1))
+    drain_halo(1)
 
 
 def finish(chunk, done, last, gain, w_in, b_in, w_out, b_out, out, tail, sems):

time: 59.4 us -> 59.2 us (level)
  no operation moved by 1% of the time
where the time goes in v4:
time: 59.2 us; the launch traced here: 59.1 us
  Pallas kernels  59.1 us (100%)
    pallas_call x1, Pallas kernels, shards(): pl.pallas_call(functools.partial(kernel, plan), out_shape=[pltpu.VMEM(tok...  56.6 us
    pallas_call x1, Pallas kernels, shards(): pl.pallas_call(functools.partial(finish, plan.chunk), out_shape=jax.Shape...  2.48 us

profile of v4, /device:TPU:0, one launch (start us, length us, event | category | flops | bytes accessed | tf_op | source)
XLA Modules:
  0.0 59.1 jit_solution(7301620951009894082)
XLA Ops:
  0.0 56.6 %shard_map.64 = (bf16[304,8192]{1,0:T(8,128)(2,1)S(1)}, bf16[304,1024]{1,0:T(8,128)(2,1)S(1)}, f32[2,304,128]{2,1,0:T(8,128)S(1)}, bf16[2,608,304]{2,1,0:T(8,128...) custom-call(bf16[304,8192]{1,0:T(8,128)(2,1)} %tokens.1, ...), custom_call_target="tpu_custom_call" | custom-call | tf_op jit(solution)/shard_map/pallas_call | solution.py:401
  56.6 2.5 %shard_map.65 = bf16[304,8192]{1,0:T(8,128)(2,1)} custom-call(bf16[304,8192]{1,0:T(8,128)(2,1)S(1)} %get-tuple-element.12.done, bf16[304,1024]{1,0:T(8,128)(2,1)S(1)} %get-tuple-element.13.last, f32[2,304,128]{2,1,0:T(8,128)S(1)} %get-tuple-element.14.gain, bf16[2,608,304]{2,1,0:T(8,128)(2,1)S(1)} %get-tuple-element.15.w_in, ...), custom_call_target="tpu_custom_call" | custom-call | tf_op jit(solution)/shard_map/pallas_call | solution.py:437

commit v5 on v4

--- a/solution.py
+++ b/solution.py
@@ -15,7 +15,7 @@
 LAG = 2
 AHEAD = 1
 HELD = 4
-STAGES = ((0, 2),)
+STAGES = ((0, 2), (4, 3), (8, 2))
 MESH = pl.DeviceIdType.MESH
 
 

time: 59.2 us -> 59.2 us (level)
  no operation moved by 1% of the time
where the time goes in v5:
time: 59.2 us; the launch traced here: 59.1 us
  Pallas kernels  59.1 us (100%)
    pallas_call x1, Pallas kernels, shards(): pl.pallas_call(functools.partial(kernel, plan), out_shape=[pltpu.VMEM(tok...  56.6 us
    pallas_call x1, Pallas kernels, shards(): pl.pallas_call(functools.partial(finish, plan.chunk), out_shape=jax.Shape...  2.48 us

profile of v5, /device:TPU:0, one launch (start us, length us, event | category | flops | bytes accessed | tf_op | source)
XLA Modules:
  0.0 59.1 jit_solution(11898770828889312234)
XLA Ops:
  0.0 56.6 %shard_map.64 = (bf16[304,8192]{1,0:T(8,128)(2,1)S(1)}, bf16[304,1024]{1,0:T(8,128)(2,1)S(1)}, f32[2,304,128]{2,1,0:T(8,128)S(1)}, bf16[2,608,304]{2,1,0:T(8,128...) custom-call(bf16[304,8192]{1,0:T(8,128)(2,1)} %tokens.1, ...), custom_call_target="tpu_custom_call" | custom-call | tf_op jit(solution)/shard_map/pallas_call | solution.py:401
  56.6 2.5 %shard_map.65 = bf16[304,8192]{1,0:T(8,128)(2,1)} custom-call(bf16[304,8192]{1,0:T(8,128)(2,1)S(1)} %get-tuple-element.12.done, bf16[304,1024]{1,0:T(8,128)(2,1)S(1)} %get-tuple-element.13.last, f32[2,304,128]{2,1,0:T(8,128)S(1)} %get-tuple-element.14.gain, bf16[2,608,304]{2,1,0:T(8,128)(2,1)S(1)} %get-tuple-element.15.w_in, ...), custom_call_target="tpu_custom_call" | custom-call | tf_op jit(solution)/shard_map/pallas_call | solution.py:437
